TPU v7x, 256 devices: a whole 4x4x8 slice. The times are simulated.
256 devices in a mesh: rcv: 32 (over z, y), hd: 8 (over x, core).
Axes of the slice: x: 4, y: 4, z: 8, core: 2. Of those that a mesh axis runs over, the one named last changes fastest.
Arguments:
- stream: bfloat16 [32768, 1024], P(('rcv', 'hd')), may hold values from -3 to 3
- queries: bfloat16 [32768, 1024], P(('rcv', 'hd')), may hold values from -9 to 9
- keys: bfloat16 [32768, 1024], P(('rcv', 'hd')), may hold values from -9 to 9
- values: bfloat16 [32768, 1024], P(('rcv', 'hd')), may hold values from -6 to 6
- out_proj: bfloat16 [1024, 1024], replicated, may hold values from -0.375 to 0.375
- norm_gain: float32 [1024], replicated, may hold values from 0.5 to 1.5
- expert_weights: bfloat16 [1024, 64, 3, 512], P(None, 'rcv'), may hold values from -0.1875 to 0.1875
- expert_ids: int32 [32768, 4], P(('rcv', 'hd')), may hold values from 0 to 63, as said below
- gate_weights: float32 [32768, 4], P(('rcv', 'hd')), may hold values from 0.1 to 1
- out_cotangent: bfloat16 [32768, 1024], P(('rcv', 'hd')), may hold values from -6 to 6
Outputs:
- block_out: bfloat16 [32768, 1024], P(('rcv', 'hd'))
- stream_grad: bfloat16 [32768, 1024], P(('rcv', 'hd'))
Inputs may be any that keep to these rules, and one draw needn't show every extreme that they name: `expert_ids`: each token names 4 different experts; its k-th id lies in k * 16 to (k + 1) * 16 - 1. Within each aligned block of 128 rows no expert is named more than 10 times, and in each of these 4 ranges one expert, the same for all blocks, is named exactly 10 times in every block.
All inputs are finite; a program needn't handle non-finite values.
Results may differ from a plain program's by a relative error of at most 0.015.
Values may be sent and summed in bfloat16 or wider, within the bound.
A program may use at most 128 MiB of HBM per device.

v0:
```python
import math
import jax
import jax.numpy as jnp
from jax import lax
from jax.sharding import PartitionSpec as P

HS = 64
NORM_EPS = 1e-06


def silu_parts(pre_gate):
    sigmoid = 1.0 / (1.0 + jnp.exp(-pre_gate))
    return (pre_gate * sigmoid, sigmoid * (1.0 + pre_gate * (1.0 - sigmoid)))


def expert_pass(arrived_rows, arrived_cot, expert_weights):
    pre_pair = jnp.einsum(
        "jmd,djcf->jmcf", arrived_rows, expert_weights[:, :, :2], preferred_element_type=jnp.float32
    )
    activated, act_slope = silu_parts(pre_pair[:, :, 0])
    up_value = pre_pair[:, :, 1]
    hidden = (activated * up_value).astype(jnp.bfloat16)
    expert_outs = jnp.einsum(
        "jmf,djf->jmd", hidden, expert_weights[:, :, 2], preferred_element_type=jnp.float32
    ).astype(jnp.bfloat16)
    back_hidden = jnp.einsum(
        "jmd,djf->jmf", arrived_cot, expert_weights[:, :, 2], preferred_element_type=jnp.float32
    )
    hidden_grads = jnp.stack(
        [back_hidden * up_value * act_slope, back_hidden * activated], axis=2
    ).astype(jnp.bfloat16)
    expert_grads = jnp.einsum(
        "jmcf,djcf->jmd", hidden_grads, expert_weights[:, :, :2], preferred_element_type=jnp.float32
    ).astype(jnp.bfloat16)
    return (expert_outs, expert_grads)


def per_device(
    stream,
    queries,
    keys,
    values,
    out_proj,
    norm_gain,
    expert_weights,
    expert_ids,
    gate_weights,
    out_cotangent,
):
    row_count, feature_width = stream.shape
    groups = lax.axis_size("rcv")
    local_count = expert_weights.shape[1]
    experts = local_count * groups
    top_count = expert_ids.shape[1]
    capacity = (5 * row_count * top_count + 4 * experts - 1) // (4 * experts)
    score_scale = 1.0 / math.sqrt(HS)
    flat_ids = expert_ids.reshape(-1)
    onehot = (flat_ids[:, None] == jnp.arange(experts, dtype=jnp.int32)[None, :]).astype(jnp.int32)
    slot_index = jnp.sum((jnp.cumsum(onehot, axis=0) - onehot) * onehot, axis=1)
    owner_rank = flat_ids // local_count
    local_expert = flat_ids % local_count
    cell_index = (local_expert * groups + owner_rank) * capacity + slot_index
    cell_total = experts * capacity
    token_index = jnp.arange(row_count * top_count, dtype=jnp.int32) // top_count
    source = jnp.full((cell_total,), row_count, jnp.int32).at[cell_index].set(token_index)

    def pack_rows(row_data):
        padded = jnp.concatenate([row_data, jnp.zeros((1, feature_width), row_data.dtype)], axis=0)
        return jnp.take(padded, source, axis=0).reshape(
            local_count, groups, capacity, feature_width
        )

    query_all, key_all, value_all = (
        lax.all_to_all(queries, "hd", split_axis=1, concat_axis=0, tiled=True),
        lax.all_to_all(keys, "hd", split_axis=1, concat_axis=0, tiled=True),
        lax.all_to_all(values, "hd", split_axis=1, concat_axis=0, tiled=True),
    )
    length = query_all.shape[0]
    head_count = query_all.shape[1] // HS
    block_rows = math.gcd(length, 512)
    key_heads = key_all.reshape(length, head_count, HS)
    value_heads = value_all.reshape(length, head_count, HS)

    def one_block(row_start):
        query_block = lax.dynamic_slice_in_dim(query_all, row_start, block_rows, 0).reshape(
            block_rows, head_count, HS
        )
        scores = (
            jnp.einsum("qhd,khd->hqk", query_block, key_heads, preferred_element_type=jnp.float32)
            * score_scale
        )
        row_max = jnp.max(scores, axis=2, keepdims=True)
        raw_weights = jnp.exp(scores - row_max)
        row_total = jnp.sum(raw_weights, axis=2)
        mixed_heads = jnp.einsum(
            "hqk,khd->qhd",
            raw_weights.astype(jnp.bfloat16),
            value_heads,
            preferred_element_type=jnp.float32,
        )
        result = mixed_heads / jnp.transpose(row_total)[:, :, None]
        return result.astype(jnp.bfloat16).reshape(block_rows, head_count * HS)

    starts = jnp.arange(length // block_rows, dtype=jnp.int32) * block_rows
    head_result = lax.map(one_block, starts).reshape(length, head_count * HS)
    attended = lax.all_to_all(head_result, "hd", split_axis=0, concat_axis=1, tiled=True)
    projected = jnp.dot(attended, out_proj, preferred_element_type=jnp.float32)
    mix_stream = (stream.astype(jnp.float32) + projected).astype(jnp.bfloat16)
    stream_wide = mix_stream.astype(jnp.float32)
    inverse = lax.rsqrt(jnp.mean(stream_wide * stream_wide, axis=1, keepdims=True) + NORM_EPS)
    normed = (norm_gain * stream_wide * inverse).astype(jnp.bfloat16)
    arrived_rows, arrived_cot = (
        lax.all_to_all(pack_rows(normed), "rcv", split_axis=1, concat_axis=1, tiled=True),
        lax.all_to_all(pack_rows(out_cotangent), "rcv", split_axis=1, concat_axis=1, tiled=True),
    )
    expert_outs, expert_grads = expert_pass(
        arrived_rows.reshape(local_count, groups * capacity, feature_width),
        arrived_cot.reshape(local_count, groups * capacity, feature_width),
        expert_weights,
    )
    back_out, back_grad = (
        lax.all_to_all(
            expert_outs.reshape(local_count, groups, capacity, feature_width),
            "rcv",
            split_axis=1,
            concat_axis=1,
            tiled=True,
        ),
        lax.all_to_all(
            expert_grads.reshape(local_count, groups, capacity, feature_width),
            "rcv",
            split_axis=1,
            concat_axis=1,
            tiled=True,
        ),
    )
    picked_out = jnp.take(back_out.reshape(cell_total, feature_width), cell_index, axis=0).reshape(
        row_count, top_count, feature_width
    )
    picked_grad = jnp.take(
        back_grad.reshape(cell_total, feature_width), cell_index, axis=0
    ).reshape(row_count, top_count, feature_width)
    gate_column = gate_weights[:, :, None]
    block_out = (
        stream_wide + jnp.sum(gate_column * picked_out.astype(jnp.float32), axis=1)
    ).astype(jnp.bfloat16)
    normed_grad = jnp.sum(gate_column * picked_grad.astype(jnp.float32), axis=1)
    weighted = norm_gain * normed_grad
    scaled = stream_wide * inverse
    stream_grad = out_cotangent.astype(jnp.float32) + inverse * (
        weighted - scaled * jnp.mean(weighted * scaled, axis=1, keepdims=True)
    )
    return (block_out, stream_grad.astype(jnp.bfloat16))


def solution(mesh):
    placed = (
        P(("rcv", "hd"), None),
        P(("rcv", "hd"), None),
        P(("rcv", "hd"), None),
        P(("rcv", "hd"), None),
        P(),
        P(),
        P(None, "rcv", None, None),
        P(("rcv", "hd"), None),
        P(("rcv", "hd"), None),
        P(("rcv", "hd"), None),
    )
    return jax.shard_map(
        per_device,
        mesh=mesh,
        in_specs=placed,
        out_specs=(P(("rcv", "hd"), None), P(("rcv", "hd"), None)),
        check_vma=False,
    )
```

profile of v0, /device:TPU:16, one launch (start us, length us, event | category | flops | bytes accessed | tf_op | source)
XLA Modules:
  0.0 263.5 jit_solution(5864382768889885304)
XLA Ops:
  0.7 1.9 copy.66
  2.6 4.4 %all-to-all-start.1 = ((bf16[128,8,128]{0,2,1:T(8,128)(2,1)}), bf16[128,8,128]{0,2,1:T(8,128)(2,1)S(1)}, u32[]{:S(2)}, u32[]{:S(2)}) async-start(bf16[128,8,128]{0,2,1:T(8,128)(2,1)} %bitcast.8), calls=%async_computation.1 | async-start | bytes 524288 | tf_op jit(solution)/shard_map/all_to_all | solution.py:75
  8.1 1.2 reduce-window.6
  10.5 4.0 %all-to-all-done.1 = bf16[128,8,128]{0,2,1:T(8,128)(2,1)S(1)} async-done(((bf16[128,8,128]{0,2,1:T(8,128)(2,1)}), bf16[128,8,128]{0,2,1:T(8,128)(2,1)S(1)}, u32[]{:S(2)}, u32[]{:S(2)}) %all-to-all-start.1) | async-done | bytes 262176 | tf_op jit(solution)/shard_map/all_to_all | solution.py:75
  14.5 3.4 %all-to-all-start.2 = ((bf16[128,8,128]{0,2,1:T(8,128)(2,1)}), bf16[128,8,128]{0,2,1:T(8,128)(2,1)S(1)}, u32[]{:S(2)}, u32[]{:S(2)}) async-start(bf16[128,8,128]{0,2,1:T(8,128)(2,1)} %bitcast.10), calls=%async_computation.2 | async-start | bytes 524288 | tf_op jit(solution)/shard_map/all_to_all | solution.py:76
  19.0 6.4 %all-to-all-done.2 = bf16[128,8,128]{0,2,1:T(8,128)(2,1)S(1)} async-done(((bf16[128,8,128]{0,2,1:T(8,128)(2,1)}), bf16[128,8,128]{0,2,1:T(8,128)(2,1)S(1)}, u32[]{:S(2)}, u32[]{:S(2)}) %all-to-all-start.2) | async-done | bytes 262176 | tf_op jit(solution)/shard_map/all_to_all | solution.py:76
  25.4 3.4 %all-to-all-start = ((bf16[128,8,128]{0,2,1:T(8,128)(2,1)}), bf16[128,8,128]{0,2,1:T(8,128)(2,1)S(1)}, u32[]{:S(2)}, u32[]{:S(2)}) async-start(bf16[128,8,128]{0,2,1:T(8,128)(2,1)} %bitcast.5), calls=%async_computation | async-start | bytes 524288 | tf_op jit(solution)/shard_map/all_to_all | solution.py:74
  28.8 2.4 scatter_custom_fusion
  32.6 3.6 %all-to-all-done = bf16[128,8,128]{0,2,1:T(8,128)(2,1)S(1)} async-done(((bf16[128,8,128]{0,2,1:T(8,128)(2,1)}), bf16[128,8,128]{0,2,1:T(8,128)(2,1)S(1)}, u32[]{:S(2)}, u32[]{:S(2)}) %all-to-all-start) | async-done | bytes 262176 | tf_op jit(solution)/shard_map/all_to_all | solution.py:74
  36.4 12.4 %while.10 = (s32[]{:T(128)}, bf16[2,512,128]{2,1,0:T(8,128)(2,1)}, s32[2]{0:T(128)S(1)}, bf16[1024,128]{1,0:T(8,128)(2,1)S(1)}, bf16[1024,2,64]{0,2,1:T(8,128)(2...) while((s32[]{:T(128)}, bf16[2,512,128]{2,1,0:T(8,128)(2,1)}, ...), condition=%wide.region_3.4_spmd, body=%wide.region_0.3_spmd.sunk | while | flops 276953088 | bytes 15487659 | solution.py:105
  40.0 0.9 fusion.70
  46.2 0.9 fusion.70
  47.2 0.9 fusion.71
  48.9 3.4 %all-to-all-start.3 = ((bf16[8,128,128]{2,1,0:T(8,128)(2,1)}), bf16[8,128,128]{2,1,0:T(8,128)(2,1)S(1)}, u32[]{:S(2)}, u32[]{:S(2)}) async-start(bf16[8,128,128]{2,1,0:T(8,128)(2,1)} %bitcast.118), calls=%async_computation.3 | async-start | bytes 524288 | tf_op jit(solution)/shard_map/all_to_all | solution.py:106
  52.4 3.5 %gather_fusion.2 = bf16[640,1024]{1,0:T(8,128)(2,1)} fusion(bf16[129,1024]{1,0:T(8,128)(2,1)S(1)} %concatenate.7, s32[1024]{0:T(1024)S(1)} %pad_clamp_fusion.1), kind=kCustom, calls=%fused_computation.2.clone | custom fusion | bytes 2624000 | tf_op jit(solution)/shard_map/jit(_take)/gather | solution.py:69
  55.9 3.9 %all-to-all-done.3 = bf16[8,128,128]{2,1,0:T(8,128)(2,1)S(1)} async-done(((bf16[8,128,128]{2,1,0:T(8,128)(2,1)}), bf16[8,128,128]{2,1,0:T(8,128)(2,1)S(1)}, u32[]{:S(2)}, u32[]{:S(2)}) %all-to-all-start.3) | async-done | bytes 262176 | tf_op jit(solution)/shard_map/all_to_all | solution.py:106
  61.5 3.5 %gather_fusion = bf16[640,1024]{1,0:T(8,128)(2,1)} fusion(bf16[129,1024]{1,0:T(8,128)(2,1)S(1)} %concatenate.6, s32[1024]{0:T(1024)S(1)} %pad_clamp_fusion.1), kind=kCustom, calls=%fused_computation.clone | custom fusion | bytes 2624000 | tf_op jit(solution)/shard_map/jit(_take)/gather | solution.py:69
  65.0 2.7 %broadcast_select_fusion.1 = (bf16[640,1024]{1,0:T(8,128)(2,1)}, bf16[640,1024]{1,0:T(8,128)(2,1)S(1)}) fusion(bf16[640,1024]{1,0:T(8,128)(2,1)} %gather_fusion, pred[640]{0:T(1024)(128)(4,1)S(1)} %compare_and_fusion, bf16[640,1024]{1,0:T(8,128)(2,1)S(1)} %copy-done.4), kind=kLoop, calls=%fused_computation.40 | loop fusion | flops 1310720 | bytes 5243520 | tf_op jit(solution)/shard_map/jit(_take)/select_n | solution.py:69
  67.7 2.4 reshape.231
  70.0 2.4 copy.78
  72.5 11.6 %all-to-all-start.4 = ((bf16[2,32,10,1024]{3,0,2,1:T(2,128)(2,1)}), bf16[2,32,10,1024]{3,0,2,1:T(2,128)(2,1)}, u32[]{:S(2)}, u32[]{:S(2)}) async-start(bf16[2,32,10,1024]{3,0,2,1:T(2,128)(2,1)} %copy.78), calls=%async_computation.4 | async-start | bytes 2621440 | tf_op jit(solution)/shard_map/all_to_all | solution.py:113
  84.6 2.4 copy.85
  87.0 30.5 %all-to-all-done.4 = bf16[2,32,10,1024]{3,0,2,1:T(2,128)(2,1)} async-done(((bf16[2,32,10,1024]{3,0,2,1:T(2,128)(2,1)}), bf16[2,32,10,1024]{3,0,2,1:T(2,128)(2,1)}, u32[]{:S(2)}, u32[]{:S(2)}) %all-to-all-start.4) | async-done | bytes 1310752 | tf_op jit(solution)/shard_map/all_to_all | solution.py:113
  117.5 5.6 %all-to-all-start.6 = ((bf16[2,32,10,1024]{3,0,2,1:T(2,128)(2,1)}), bf16[2,32,10,1024]{3,0,2,1:T(2,128)(2,1)}, u32[]{:S(2)}, u32[]{:S(2)}) async-start(bf16[2,32,10,1024]{3,0,2,1:T(2,128)(2,1)} %copy.85), calls=%async_computation.6 | async-start | bytes 2621440 | tf_op jit(solution)/shard_map/all_to_all | solution.py:114
  123.1 5.1 %slice.22 = bf16[1024,2,2,512]{3,1,2,0:T(2,128)(2,1)S(1)} slice(bf16[1024,2,3,512]{3,1,2,0:T(2,128)(2,1)} %param.22), slice={[0:1024], [0:2], [0:2], [0:512]} | slice | bytes 8388608 | tf_op jit(solution)/shard_map/slice | solution.py:18
  128.2 4.5 %slice.25 = bf16[1024,2,1,512]{3,1,2,0:T(2,128)(2,1)S(1)} slice(bf16[1024,2,3,512]{3,1,2,0:T(2,128)(2,1)} %param.22), slice={[0:1024], [0:2], [2:3], [0:512]} | slice | bytes 4194304 | tf_op jit(solution)/shard_map/slice | solution.py:24
  132.8 5.6 %fusion.16 = f32[2,320,2,512]{3,1,2,0:T(8,128)} fusion(bf16[1024,2,2,512]{3,1,2,0:T(2,128)(2,1)S(1)} %slice.22, bf16[2,320,1024,1]{2,0,1,3:T(2,128)(2,1)} %bitcast.19), kind=kOutput, calls=%fused_computation.18 | convolution fusion | flops 1342177280 | bytes 8126464 | tf_op jit(solution)/shard_map/jmd,djcf->jmcf/dot_general | solution.py:17
  138.3 17.2 %all-to-all-done.6 = bf16[2,32,10,1024]{3,0,2,1:T(2,128)(2,1)} async-done(((bf16[2,32,10,1024]{3,0,2,1:T(2,128)(2,1)}), bf16[2,32,10,1024]{3,0,2,1:T(2,128)(2,1)}, u32[]{:S(2)}, u32[]{:S(2)}) %all-to-all-start.6) | async-done | bytes 1310752 | tf_op jit(solution)/shard_map/all_to_all | solution.py:114
  155.6 3.6 %fusion.32 = (bf16[2,320,1,512]{3,1,0,2:T(8,128)(2,1)S(1)}, bf16[2,320,1,512]{3,1,0,2:T(8,128)(2,1)S(1)}) fusion(f32[2,320,2,512]{3,1,2,0:T(8,128)} %fusion.16, bf16[1024,2,1,512]{3,1,2,0:T(2,128)(2,1)S(1)} %slice.25, bf16[2,320,1024]{2,0,1:T(2,128)(2,1)} %bitcast.24), kind=kOutput, calls=%fused_computation.47 | convolution fusion | flops 675348480 | bytes 7340032 | tf_op jit(solution)/shard_map/jmd,djf->jmf/dot_general | solution.py:26
  159.2 1.7 bitcast_convert_fusion
  160.9 2.4 copy.88
  163.3 5.6 %all-to-all-start.7 = ((bf16[2,32,10,1024]{3,0,2,1:T(2,128)(2,1)}), bf16[2,32,10,1024]{3,0,2,1:T(2,128)(2,1)S(1)}, u32[]{:S(2)}, u32[]{:S(2)}) async-start(bf16[2,32,10,1024]{3,0,2,1:T(2,128)(2,1)} %bitcast.28), calls=%async_computation.7 | async-start | bytes 2621440 | tf_op jit(solution)/shard_map/all_to_all | solution.py:129
  168.9 3.3 %fusion.22 = bf16[2,320,1024]{2,1,0:T(8,128)(2,1)S(1)} fusion(bf16[1024,2,1,512]{3,1,2,0:T(2,128)(2,1)} %copy-done.7, f32[2,320,2,512]{3,1,2,0:T(8,128)} %fusion.16), kind=kOutput, calls=%fused_computation.26 | convolution fusion | flops 673710080 | bytes 6029312 | tf_op jit(solution)/shard_map/jmf,djf->jmd/dot_general | solution.py:23
  172.2 2.4 copy.83
  174.6 25.8 %all-to-all-done.7 = bf16[2,32,10,1024]{3,0,2,1:T(2,128)(2,1)S(1)} async-done(((bf16[2,32,10,1024]{3,0,2,1:T(2,128)(2,1)}), bf16[2,32,10,1024]{3,0,2,1:T(2,128)(2,1)S(1)}, u32[]{:S(2)}, u32[]{:S(2)}) %all-to-all-start.7) | async-done | bytes 1310752 | tf_op jit(solution)/shard_map/all_to_all | solution.py:129
  200.4 6.1 %all-to-all-start.5 = ((bf16[2,32,10,1024]{3,0,2,1:T(2,128)(2,1)}), bf16[2,32,10,1024]{3,0,2,1:T(2,128)(2,1)S(1)}, u32[]{:S(2)}, u32[]{:S(2)}) async-start(bf16[2,32,10,1024]{3,0,2,1:T(2,128)(2,1)} %bitcast.23), calls=%async_computation.5 | async-start | bytes 2621440 | tf_op jit(solution)/shard_map/all_to_all | solution.py:122
  206.7 1.9 copy.89
  208.5 2.6 reshape.238
  211.1 27.4 %all-to-all-done.5 = bf16[2,32,10,1024]{3,0,2,1:T(2,128)(2,1)S(1)} async-done(((bf16[2,32,10,1024]{3,0,2,1:T(2,128)(2,1)}), bf16[2,32,10,1024]{3,0,2,1:T(2,128)(2,1)S(1)}, u32[]{:S(2)}, u32[]{:S(2)}) %all-to-all-start.5) | async-done | bytes 1310752 | tf_op jit(solution)/shard_map/all_to_all | solution.py:122
  238.5 1.9 copy.84
  240.4 2.6 reshape.234
  243.0 2.8 %gather_fusion.3 = bf16[512,1024]{1,0:T(8,128)(2,1)} fusion(bf16[640,1024]{1,0:T(8,128)(2,1)S(1)} %reshape.238, s32[1024]{0:T(1024)S(1)} %pad_clamp_fusion), kind=kCustom, calls=%fused_computation.3.clone | custom fusion | bytes 2099200 | tf_op jit(solution)/shard_map/jit(_take)/gather | solution.py:140
  245.7 2.8 %gather_fusion.1 = bf16[512,1024]{1,0:T(8,128)(2,1)} fusion(bf16[640,1024]{1,0:T(8,128)(2,1)S(1)} %reshape.234, s32[1024]{0:T(1024)S(1)} %pad_clamp_fusion), kind=kCustom, calls=%fused_computation.1.clone | custom fusion | bytes 2099200 | tf_op jit(solution)/shard_map/jit(_take)/gather | solution.py:137
  248.5 3.2 %select_convert_fusion.1 = (f32[512,1024]{1,0:T(8,128)}, f32[512,1024]{1,0:T(8,128)S(1)}) fusion(bf16[512,1024]{1,0:T(8,128)(2,1)} %gather_fusion.1, pred[512]{0:T(512)(128)(4,1)S(1)} %get-tuple-element.57, bf16[512,1024]{1,0:T(8,128)(2,1)} %gather_fusion.3), kind=kLoop, calls=%fused_computation.45 | loop fusion | flops 2097152 | bytes 6291968 | tf_op jit(solution)/shard_map/convert_element_type | solution.py:145
  251.7 2.8 %reshape.239 = f32[128,4,1024]{2,1,0:T(4,128)} reshape(f32[512,1024]{1,0:T(8,128)} %get-tuple-element.67) | data formatting | bytes 4194304 | tf_op jit(solution)/shard_map/convert_element_type | solution.py:145
  254.6 1.6 reshape.240
  256.2 5.5 %multiply_reduce_fusion.1 = (f32[128,1024]{1,0:T(8,128)S(1)}, f32[128,1024]{1,0:T(8,128)S(1)}) fusion(f32[128,4,1024]{2,1,0:T(4,128)} %reshape.240, f32[128,4]{1,0:T(8,128)S(1)} %copy.73, f32[128,4,1024]{2,1,0:T(4,128)} %reshape.239), kind=kLoop, calls=%fused_computation.22 | loop fusion | flops 1835008 | bytes 5244928 | tf_op jit(solution)/shard_map/reduce_sum | solution.py:147
  262.0 1.0 add_convert_fusion
  (82 shorter events, 13.5 us)
Async XLA Ops:
  0.6 59.3 %copy-start = (bf16[1024,1024]{1,0:T(8,128)(2,1)S(1)}, bf16[1024,1024]{1,0:T(8,128)(2,1)}, u32[]{:S(2)}) copy-start(bf16[1024,1024]{1,0:T(8,128)(2,1)} %param.20) | copy-start | bytes 6291460
  0.6 8.9 %copy-start.10 = (bf16[128,1024]{1,0:T(8,128)(2,1)S(1)}, bf16[128,1024]{1,0:T(8,128)(2,1)}, u32[]{:S(2)}) copy-start(bf16[128,1024]{1,0:T(8,128)(2,1)} %param.19) | copy-start | bytes 786436
  2.6 15.5 %copy-start.11 = (bf16[128,1024]{1,0:T(8,128)(2,1)S(1)}, bf16[128,1024]{1,0:T(8,128)(2,1)}, u32[]{:S(2)}) copy-start(bf16[128,1024]{1,0:T(8,128)(2,1)} %param.17) | copy-start | bytes 786436
  2.6 11.9 %all-to-all-start.1 = ((bf16[128,8,128]{0,2,1:T(8,128)(2,1)}), bf16[128,8,128]{0,2,1:T(8,128)(2,1)S(1)}, u32[]{:S(2)}, u32[]{:S(2)}) async-start(bf16[128,8,128]{0,2,1:T(8,128)(2,1)} %bitcast.8), calls=%async_computation.1 | async-start | bytes 524288 | tf_op jit(solution)/shard_map/all_to_all | solution.py:75
  14.5 10.8 %all-to-all-start.2 = ((bf16[128,8,128]{0,2,1:T(8,128)(2,1)}), bf16[128,8,128]{0,2,1:T(8,128)(2,1)S(1)}, u32[]{:S(2)}, u32[]{:S(2)}) async-start(bf16[128,8,128]{0,2,1:T(8,128)(2,1)} %bitcast.10), calls=%async_computation.2 | async-start | bytes 524288 | tf_op jit(solution)/shard_map/all_to_all | solution.py:76
  25.4 10.9 %all-to-all-start = ((bf16[128,8,128]{0,2,1:T(8,128)(2,1)}), bf16[128,8,128]{0,2,1:T(8,128)(2,1)S(1)}, u32[]{:S(2)}, u32[]{:S(2)}) async-start(bf16[128,8,128]{0,2,1:T(8,128)(2,1)} %bitcast.5), calls=%async_computation | async-start | bytes 524288 | tf_op jit(solution)/shard_map/all_to_all | solution.py:74
  36.4 15.9 %copy-start.8 = (bf16[128,1024]{1,0:T(8,128)(2,1)S(1)}, bf16[128,1024]{1,0:T(8,128)(2,1)}, u32[]{:S(2)}) copy-start(bf16[128,1024]{1,0:T(8,128)(2,1)} %param.25) | copy-start | bytes 786436
  40.0 1.0 copy-start.12
  46.2 1.0 copy-start.12
  48.9 10.9 %all-to-all-start.3 = ((bf16[8,128,128]{2,1,0:T(8,128)(2,1)}), bf16[8,128,128]{2,1,0:T(8,128)(2,1)S(1)}, u32[]{:S(2)}, u32[]{:S(2)}) async-start(bf16[8,128,128]{2,1,0:T(8,128)(2,1)} %bitcast.118), calls=%async_computation.3 | async-start | bytes 524288 | tf_op jit(solution)/shard_map/all_to_all | solution.py:106
  52.4 7.6 %copy-start.13 = (bf16[128,1024]{1,0:T(8,128)(2,1)S(1)}, bf16[128,1024]{1,0:T(8,128)(2,1)}, u32[]{:S(2)}) copy-start(bf16[128,1024]{1,0:T(8,128)(2,1)} %param.16) | copy-start | bytes 786436
  59.9 1.4 copy-start.14
  60.5 0.9 copy-start.2
  61.5 3.5 %copy-start.4 = (bf16[640,1024]{1,0:T(8,128)(2,1)S(1)}, bf16[640,1024]{1,0:T(8,128)(2,1)}, u32[]{:S(2)}) copy-start(bf16[640,1024]{1,0:T(8,128)(2,1)} %gather_fusion.2) | copy-start | bytes 3932164
  72.5 45.0 %all-to-all-start.4 = ((bf16[2,32,10,1024]{3,0,2,1:T(2,128)(2,1)}), bf16[2,32,10,1024]{3,0,2,1:T(2,128)(2,1)}, u32[]{:S(2)}, u32[]{:S(2)}) async-start(bf16[2,32,10,1024]{3,0,2,1:T(2,128)(2,1)} %copy.78), calls=%async_computation.4 | async-start | bytes 2621440 | tf_op jit(solution)/shard_map/all_to_all | solution.py:113
  117.5 38.1 %all-to-all-start.6 = ((bf16[2,32,10,1024]{3,0,2,1:T(2,128)(2,1)}), bf16[2,32,10,1024]{3,0,2,1:T(2,128)(2,1)}, u32[]{:S(2)}, u32[]{:S(2)}) async-start(bf16[2,32,10,1024]{3,0,2,1:T(2,128)(2,1)} %copy.85), calls=%async_computation.6 | async-start | bytes 2621440 | tf_op jit(solution)/shard_map/all_to_all | solution.py:114
  128.2 4.6 %copy-start.5 = (bf16[1024,2,2,512]{3,1,2,0:T(2,128)(2,1)}, bf16[1024,2,2,512]{3,1,2,0:T(2,128)(2,1)S(1)}, u32[]{:S(2)}) copy-start(bf16[1024,2,2,512]{3,1,2,0:T(2,128)(2,1)S(1)} %slice.22) | copy-start | bytes 12582916
  132.8 22.8 %copy-start.7 = (bf16[1024,2,1,512]{3,1,2,0:T(2,128)(2,1)}, bf16[1024,2,1,512]{3,1,2,0:T(2,128)(2,1)S(1)}, u32[]{:S(2)}) copy-start(bf16[1024,2,1,512]{3,1,2,0:T(2,128)(2,1)S(1)} %slice.25) | copy-start | bytes 6291460
  155.6 3.6 %copy-start.6 = (bf16[1024,2,2,512]{3,1,2,0:T(2,128)(2,1)S(1)}, bf16[1024,2,2,512]{3,1,2,0:T(2,128)(2,1)}, u32[]{:S(2)}) copy-start(bf16[1024,2,2,512]{3,1,2,0:T(2,128)(2,1)} %copy-done.5) | copy-start | bytes 12582916
  163.3 37.1 %all-to-all-start.7 = ((bf16[2,32,10,1024]{3,0,2,1:T(2,128)(2,1)}), bf16[2,32,10,1024]{3,0,2,1:T(2,128)(2,1)S(1)}, u32[]{:S(2)}, u32[]{:S(2)}) async-start(bf16[2,32,10,1024]{3,0,2,1:T(2,128)(2,1)} %bitcast.28), calls=%async_computation.7 | async-start | bytes 2621440 | tf_op jit(solution)/shard_map/all_to_all | solution.py:129
  200.4 6.1 %copy-start.15 = (f32[128,4]{0,1:T(4,128)S(1)}, f32[128,4]{0,1:T(4,128)}, u32[]{:S(2)}) copy-start(f32[128,4]{0,1:T(4,128)} %param.24) | copy-start | bytes 6148
  200.4 38.1 %all-to-all-start.5 = ((bf16[2,32,10,1024]{3,0,2,1:T(2,128)(2,1)}), bf16[2,32,10,1024]{3,0,2,1:T(2,128)(2,1)S(1)}, u32[]{:S(2)}, u32[]{:S(2)}) async-start(bf16[2,32,10,1024]{3,0,2,1:T(2,128)(2,1)} %bitcast.23), calls=%async_computation.5 | async-start | bytes 2621440 | tf_op jit(solution)/shard_map/all_to_all | solution.py:122
  256.2 5.5 %copy-start.3 = (f32[128,1024]{1,0:T(8,128)S(1)}, f32[128,1024]{1,0:T(8,128)}, u32[]{:S(2)}) copy-start(f32[128,1024]{1,0:T(8,128)} %copy-done.2) | copy-start | bytes 1572868
  256.2 5.7 %copy-start.9 = (bf16[128,1024]{1,0:T(8,128)(2,1)S(1)}, bf16[128,1024]{1,0:T(8,128)(2,1)}, u32[]{:S(2)}) copy-start(bf16[128,1024]{1,0:T(8,128)(2,1)} %param.25) | copy-start | bytes 786436
  261.7 1.8 copy-start.1
where the time goes:
time: 265 us; the launch traced here: 264 us
  waiting for transfers between devices  119 us (45%)
  local copies, waits for them, and re-layouts  61.7 us (23%)
  starting transfers between devices  43.6 us (16%)
  matrix products  18.2 us (7%)
  other arithmetic  16 us (6%)
  loops' own time  3.97 us (1%)
    all_to_all x1, waiting for transfers between devices, per_device(): lax.all_to_all(pack_rows(normed), 'rcv', split_axis=1, concat_axis=1, til...  30.5 us
    all_to_all x1, waiting for transfers between devices, per_device(): lax.all_to_all(expert_outs.reshape(local_count, groups, capacity, feature...  27.4 us
    all_to_all x1, waiting for transfers between devices, per_device(): lax.all_to_all(expert_grads.reshape(local_count, groups, capacity, featur...  25.8 us
    all_to_all x1, waiting for transfers between devices, per_device(): lax.all_to_all(pack_rows(out_cotangent), 'rcv', split_axis=1, concat_axis...  17.2 us
    all_to_all x1, starting transfers between devices, per_device(): lax.all_to_all(pack_rows(normed), 'rcv', split_axis=1, concat_axis=1, til...  11.6 us
    reshape x4, local copies, waits for them, and re-layouts, pack_rows(): jnp.take(padded, source, axis=0)  7.68 us
    gather x2, local copies, waits for them, and re-layouts, pack_rows(): jnp.take(padded, source, axis=0)  6.95 us
    all_to_all x1, waiting for transfers between devices, per_device(): lax.all_to_all(values, 'hd', split_axis=1, concat_axis=0, tiled=True)  6.43 us
  transfers between devices with their start and end apart: 8, of which 8 were waited for; matrix products, arithmetic and copies ran while one was open for 15% of the time, Pallas kernels for 0%

commit v1 on v0

--- a/solution.py
+++ b/solution.py
@@ -3,6 +3,7 @@
 import jax.numpy as jnp
 from jax import lax
 from jax.sharding import PartitionSpec as P
+from jax.lax import all_to_all, psum
 
 HS = 64
 NORM_EPS = 1e-06
@@ -110,7 +111,12 @@
     inverse = lax.rsqrt(jnp.mean(stream_wide * stream_wide, axis=1, keepdims=True) + NORM_EPS)
     normed = (norm_gain * stream_wide * inverse).astype(jnp.bfloat16)
     arrived_rows, arrived_cot = (
-        lax.all_to_all(pack_rows(normed), "rcv", split_axis=1, concat_axis=1, tiled=True),
+        jnp.concatenate(
+            all_to_all(
+                jnp.stack(jnp.split(pack_rows(normed), psum(1, "rcv"), axis=1)), "rcv", 0, 0
+            ),
+            axis=1,
+        ),
         lax.all_to_all(pack_rows(out_cotangent), "rcv", split_axis=1, concat_axis=1, tiled=True),
     )
     expert_outs, expert_grads = expert_pass(

time: 265 us -> 265 us (level)
    reshape x4 -> x3, local copies, waits for them, and re-layouts: 7.68 us -> 5.24 us  [pack_rows(): jnp.take(padded, source, axis=0)]
    unnamed x35 -> x64, local copies, waits for them, and re-layouts: 5.98 us -> 6.59 us
  transfers between devices with their start and end apart: 8 -> 8, of which waited for: 8 -> 8; matrix products, arithmetic and copies ran while one was open for 15% -> 16% of each run, Pallas kernels for 0% -> 0%
where the time goes in v1:
time: 265 us; the launch traced here: 263 us
  waiting for transfers between devices  118 us (45%)
  local copies, waits for them, and re-layouts  62.3 us (24%)
  starting transfers between devices  42.9 us (16%)
  matrix products  18.2 us (7%)
  other arithmetic  16.1 us (6%)
  loops' own time  3.97 us (1%)
    all_to_all x1, waiting for transfers between devices, per_device(): all_to_all(jnp.stack(jnp.split(pack_rows(normed), psum(1, 'rcv'), axis=1)...  30.5 us
    all_to_all x1, waiting for transfers between devices, per_device(): lax.all_to_all(expert_outs.reshape(local_count, groups, capacity, feature...  27.4 us
    all_to_all x1, waiting for transfers between devices, per_device(): lax.all_to_all(expert_grads.reshape(local_count, groups, capacity, featur...  26.2 us
    all_to_all x1, waiting for transfers between devices, per_device(): lax.all_to_all(pack_rows(out_cotangent), 'rcv', split_axis=1, concat_axis...  17.2 us
    all_to_all x1, starting transfers between devices, per_device(): all_to_all(jnp.stack(jnp.split(pack_rows(normed), psum(1, 'rcv'), axis=1)...  11.6 us
    gather x2, local copies, waits for them, and re-layouts, pack_rows(): jnp.take(padded, source, axis=0)  6.95 us
    unnamed x64, local copies, waits for them, and re-layouts  6.59 us
    all_to_all x1, waiting for transfers between devices, per_device(): lax.all_to_all(values, 'hd', split_axis=1, concat_axis=0, tiled=True)  6.43 us
  transfers between devices with their start and end apart: 8, of which 8 were waited for; matrix products, arithmetic and copies ran while one was open for 16% of the time, Pallas kernels for 0%

profile of v1, /device:TPU:16, one launch (start us, length us, event | category | flops | bytes accessed | tf_op | source)
XLA Modules:
  0.0 263.2 jit_solution(12703323422584909223)
XLA Ops:
  0.7 1.9 copy.160
  2.6 4.3 %all-to-all-start.1 = ((bf16[128,8,128]{0,2,1:T(8,128)(2,1)}), bf16[128,8,128]{0,2,1:T(8,128)(2,1)S(1)}, u32[]{:S(2)}, u32[]{:S(2)}) async-start(bf16[128,8,128]{0,2,1:T(8,128)(2,1)} %bitcast.8), calls=%async_computation.1 | async-start | bytes 524288 | tf_op jit(solution)/shard_map/all_to_all | solution.py:76
  7.9 1.2 reduce-window.6
  9.4 1.8 copy.162
  11.3 3.1 %all-to-all-done.1 = bf16[128,8,128]{0,2,1:T(8,128)(2,1)S(1)} async-done(((bf16[128,8,128]{0,2,1:T(8,128)(2,1)}), bf16[128,8,128]{0,2,1:T(8,128)(2,1)S(1)}, u32[]{:S(2)}, u32[]{:S(2)}) %all-to-all-start.1) | async-done | bytes 262176 | tf_op jit(solution)/shard_map/all_to_all | solution.py:76
  14.4 3.4 %all-to-all-start.2 = ((bf16[128,8,128]{0,2,1:T(8,128)(2,1)}), bf16[128,8,128]{0,2,1:T(8,128)(2,1)S(1)}, u32[]{:S(2)}, u32[]{:S(2)}) async-start(bf16[128,8,128]{0,2,1:T(8,128)(2,1)} %bitcast.10), calls=%async_computation.2 | async-start | bytes 524288 | tf_op jit(solution)/shard_map/all_to_all | solution.py:77
  18.8 6.4 %all-to-all-done.2 = bf16[128,8,128]{0,2,1:T(8,128)(2,1)S(1)} async-done(((bf16[128,8,128]{0,2,1:T(8,128)(2,1)}), bf16[128,8,128]{0,2,1:T(8,128)(2,1)S(1)}, u32[]{:S(2)}, u32[]{:S(2)}) %all-to-all-start.2) | async-done | bytes 262176 | tf_op jit(solution)/shard_map/all_to_all | solution.py:77
  25.3 3.4 %all-to-all-start = ((bf16[128,8,128]{0,2,1:T(8,128)(2,1)}), bf16[128,8,128]{0,2,1:T(8,128)(2,1)S(1)}, u32[]{:S(2)}, u32[]{:S(2)}) async-start(bf16[128,8,128]{0,2,1:T(8,128)(2,1)} %bitcast.5), calls=%async_computation | async-start | bytes 524288 | tf_op jit(solution)/shard_map/all_to_all | solution.py:75
  28.7 2.4 scatter_custom_fusion
  32.5 3.7 %all-to-all-done = bf16[128,8,128]{0,2,1:T(8,128)(2,1)S(1)} async-done(((bf16[128,8,128]{0,2,1:T(8,128)(2,1)}), bf16[128,8,128]{0,2,1:T(8,128)(2,1)S(1)}, u32[]{:S(2)}, u32[]{:S(2)}) %all-to-all-start) | async-done | bytes 262176 | tf_op jit(solution)/shard_map/all_to_all | solution.py:75
  36.3 12.5 %while.10 = (s32[]{:T(128)}, bf16[2,512,128]{2,1,0:T(8,128)(2,1)}, s32[2]{0:T(128)S(1)}, bf16[1024,128]{1,0:T(8,128)(2,1)S(1)}, bf16[1024,2,64]{0,2,1:T(8,128)(2...) while((s32[]{:T(128)}, bf16[2,512,128]{2,1,0:T(8,128)(2,1)}, ...), condition=%wide.region_3.4_spmd, body=%wide.region_0.3_spmd.sunk | while | flops 276953088 | bytes 15487659 | solution.py:106
  39.9 0.9 fusion.102
  46.1 0.9 fusion.102
  48.8 3.4 %all-to-all-start.3 = ((bf16[8,128,128]{2,1,0:T(8,128)(2,1)}), bf16[8,128,128]{2,1,0:T(8,128)(2,1)S(1)}, u32[]{:S(2)}, u32[]{:S(2)}) async-start(bf16[8,128,128]{2,1,0:T(8,128)(2,1)} %bitcast.310), calls=%async_computation.3 | async-start | bytes 524288 | tf_op jit(solution)/shard_map/all_to_all | solution.py:107
  52.2 3.5 %gather_fusion.2 = bf16[640,1024]{1,0:T(8,128)(2,1)} fusion(bf16[129,1024]{1,0:T(8,128)(2,1)S(1)} %concatenate.7, s32[1024]{0:T(1024)S(1)} %pad_clamp_fusion.1), kind=kCustom, calls=%fused_computation.2.clone | custom fusion | bytes 2624000 | tf_op jit(solution)/shard_map/jit(_take)/gather | solution.py:70
  55.7 3.9 %all-to-all-done.3 = bf16[8,128,128]{2,1,0:T(8,128)(2,1)S(1)} async-done(((bf16[8,128,128]{2,1,0:T(8,128)(2,1)}), bf16[8,128,128]{2,1,0:T(8,128)(2,1)S(1)}, u32[]{:S(2)}, u32[]{:S(2)}) %all-to-all-start.3) | async-done | bytes 262176 | tf_op jit(solution)/shard_map/all_to_all | solution.py:107
  61.4 3.5 %gather_fusion = bf16[640,1024]{1,0:T(8,128)(2,1)} fusion(bf16[129,1024]{1,0:T(8,128)(2,1)S(1)} %concatenate.6, s32[1024]{0:T(1024)S(1)} %pad_clamp_fusion.1), kind=kCustom, calls=%fused_computation.clone | custom fusion | bytes 2624000 | tf_op jit(solution)/shard_map/jit(_take)/gather | solution.py:70
  64.8 2.7 %broadcast_select_fusion.1 = (bf16[640,1024]{1,0:T(8,128)(2,1)}, bf16[640,1024]{1,0:T(8,128)(2,1)S(1)}) fusion(bf16[640,1024]{1,0:T(8,128)(2,1)} %gather_fusion, pred[640]{0:T(1024)(128)(4,1)S(1)} %compare_and_fusion, bf16[640,1024]{1,0:T(8,128)(2,1)S(1)} %copy-done.4), kind=kLoop, calls=%fused_computation.40 | loop fusion | flops 1310720 | bytes 5243520 | tf_op jit(solution)/shard_map/jit(_take)/select_n | solution.py:70
  67.5 2.4 reshape.231
  70.3 2.4 copy.203
  72.8 11.6 %all-to-all-start.4 = ((bf16[32,2,1,10,1024]{4,1,3,2,0:T(2,128)(2,1)}), bf16[32,2,1,10,1024]{4,1,3,2,0:T(2,128)(2,1)}, u32[]{:S(2)}, u32[]{:S(2)}) async-start(bf16[32,2,1,10,1024]{4,1,3,2,0:T(2,128)(2,1)} %copy.203), calls=%async_computation.4 | async-start | bytes 2621440 | tf_op jit(solution)/shard_map/all_to_all | solution.py:115
  84.9 2.4 copy.210
  87.3 30.5 %all-to-all-done.4 = bf16[32,2,1,10,1024]{4,1,3,2,0:T(2,128)(2,1)} async-done(((bf16[32,2,1,10,1024]{4,1,3,2,0:T(2,128)(2,1)}), bf16[32,2,1,10,1024]{4,1,3,2,0:T(2,128)(2,1)}, u32[]{:S(2)}, u32[]{:S(2)}) %all-to-all-start.4) | async-done | bytes 1310752 | tf_op jit(solution)/shard_map/all_to_all | solution.py:115
  117.8 5.6 %all-to-all-start.6 = ((bf16[2,32,10,1024]{3,0,2,1:T(2,128)(2,1)}), bf16[2,32,10,1024]{3,0,2,1:T(2,128)(2,1)}, u32[]{:S(2)}, u32[]{:S(2)}) async-start(bf16[2,32,10,1024]{3,0,2,1:T(2,128)(2,1)} %copy.210), calls=%async_computation.6 | async-start | bytes 2621440 | tf_op jit(solution)/shard_map/all_to_all | solution.py:120
  123.4 5.1 %slice.22 = bf16[1024,2,2,512]{3,1,2,0:T(2,128)(2,1)S(1)} slice(bf16[1024,2,3,512]{3,1,2,0:T(2,128)(2,1)} %param.22), slice={[0:1024], [0:2], [0:2], [0:512]} | slice | bytes 8388608 | tf_op jit(solution)/shard_map/slice | solution.py:19
  128.5 4.5 %slice.25 = bf16[1024,2,1,512]{3,1,2,0:T(2,128)(2,1)S(1)} slice(bf16[1024,2,3,512]{3,1,2,0:T(2,128)(2,1)} %param.22), slice={[0:1024], [0:2], [2:3], [0:512]} | slice | bytes 4194304 | tf_op jit(solution)/shard_map/slice | solution.py:25
  133.1 5.6 %fusion.16 = f32[2,320,2,512]{3,1,2,0:T(8,128)} fusion(bf16[1024,2,2,512]{3,1,2,0:T(2,128)(2,1)S(1)} %slice.22, bf16[2,320,1024,1]{2,0,1,3:T(2,128)(2,1)} %bitcast.52), kind=kOutput, calls=%fused_computation.18 | convolution fusion | flops 1342177280 | bytes 8126464 | tf_op jit(solution)/shard_map/jmd,djcf->jmcf/dot_general | solution.py:18
  138.7 17.2 %all-to-all-done.6 = bf16[2,32,10,1024]{3,0,2,1:T(2,128)(2,1)} async-done(((bf16[2,32,10,1024]{3,0,2,1:T(2,128)(2,1)}), bf16[2,32,10,1024]{3,0,2,1:T(2,128)(2,1)}, u32[]{:S(2)}, u32[]{:S(2)}) %all-to-all-start.6) | async-done | bytes 1310752 | tf_op jit(solution)/shard_map/all_to_all | solution.py:120
  155.9 3.6 %fusion.32 = (bf16[2,320,1,512]{3,1,0,2:T(8,128)(2,1)S(1)}, bf16[2,320,1,512]{3,1,0,2:T(8,128)(2,1)S(1)}) fusion(f32[2,320,2,512]{3,1,2,0:T(8,128)} %fusion.16, bf16[1024,2,1,512]{3,1,2,0:T(2,128)(2,1)S(1)} %slice.25, bf16[2,320,1024]{2,0,1:T(2,128)(2,1)} %bitcast.57), kind=kOutput, calls=%fused_computation.47 | convolution fusion | flops 675348480 | bytes 7340032 | tf_op jit(solution)/shard_map/jmd,djf->jmf/dot_general | solution.py:27
  159.5 1.7 bitcast_convert_fusion
  161.2 2.4 copy.213
  163.6 5.6 %all-to-all-start.7 = ((bf16[2,32,10,1024]{3,0,2,1:T(2,128)(2,1)}), bf16[2,32,10,1024]{3,0,2,1:T(2,128)(2,1)S(1)}, u32[]{:S(2)}, u32[]{:S(2)}) async-start(bf16[2,32,10,1024]{3,0,2,1:T(2,128)(2,1)} %bitcast.61), calls=%async_computation.7 | async-start | bytes 2621440 | tf_op jit(solution)/shard_map/all_to_all | solution.py:135
  169.2 3.3 %fusion.22 = bf16[2,320,1024]{2,1,0:T(8,128)(2,1)S(1)} fusion(bf16[1024,2,1,512]{3,1,2,0:T(2,128)(2,1)} %copy-done.7, f32[2,320,2,512]{3,1,2,0:T(8,128)} %fusion.16), kind=kOutput, calls=%fused_computation.26 | convolution fusion | flops 673710080 | bytes 6029312 | tf_op jit(solution)/shard_map/jmf,djf->jmd/dot_general | solution.py:24
  172.5 2.4 copy.208
  174.9 26.2 %all-to-all-done.7 = bf16[2,32,10,1024]{3,0,2,1:T(2,128)(2,1)S(1)} async-done(((bf16[2,32,10,1024]{3,0,2,1:T(2,128)(2,1)}), bf16[2,32,10,1024]{3,0,2,1:T(2,128)(2,1)S(1)}, u32[]{:S(2)}, u32[]{:S(2)}) %all-to-all-start.7) | async-done | bytes 1310752 | tf_op jit(solution)/shard_map/all_to_all | solution.py:135
  201.1 5.6 %all-to-all-start.5 = ((bf16[2,32,10,1024]{3,0,2,1:T(2,128)(2,1)}), bf16[2,32,10,1024]{3,0,2,1:T(2,128)(2,1)S(1)}, u32[]{:S(2)}, u32[]{:S(2)}) async-start(bf16[2,32,10,1024]{3,0,2,1:T(2,128)(2,1)} %bitcast.56), calls=%async_computation.5 | async-start | bytes 2621440 | tf_op jit(solution)/shard_map/all_to_all | solution.py:128
  206.8 1.9 copy.214
  208.7 2.6 reshape.238
  211.3 27.4 %all-to-all-done.5 = bf16[2,32,10,1024]{3,0,2,1:T(2,128)(2,1)S(1)} async-done(((bf16[2,32,10,1024]{3,0,2,1:T(2,128)(2,1)}), bf16[2,32,10,1024]{3,0,2,1:T(2,128)(2,1)S(1)}, u32[]{:S(2)}, u32[]{:S(2)}) %all-to-all-start.5) | async-done | bytes 1310752 | tf_op jit(solution)/shard_map/all_to_all | solution.py:128
  238.7 1.9 copy.209
  240.5 2.6 reshape.234
  243.1 2.8 %gather_fusion.3 = bf16[512,1024]{1,0:T(8,128)(2,1)} fusion(bf16[640,1024]{1,0:T(8,128)(2,1)S(1)} %reshape.238, s32[1024]{0:T(1024)S(1)} %pad_clamp_fusion), kind=kCustom, calls=%fused_computation.3.clone | custom fusion | bytes 2099200 | tf_op jit(solution)/shard_map/jit(_take)/gather | solution.py:146
  245.9 2.8 %gather_fusion.1 = bf16[512,1024]{1,0:T(8,128)(2,1)} fusion(bf16[640,1024]{1,0:T(8,128)(2,1)S(1)} %reshape.234, s32[1024]{0:T(1024)S(1)} %pad_clamp_fusion), kind=kCustom, calls=%fused_computation.1.clone | custom fusion | bytes 2099200 | tf_op jit(solution)/shard_map/jit(_take)/gather | solution.py:143
  248.7 3.2 %select_convert_fusion.1 = (f32[512,1024]{1,0:T(8,128)}, f32[512,1024]{1,0:T(8,128)S(1)}) fusion(bf16[512,1024]{1,0:T(8,128)(2,1)} %gather_fusion.1, pred[512]{0:T(512)(128)(4,1)S(1)} %get-tuple-element.57, bf16[512,1024]{1,0:T(8,128)(2,1)} %gather_fusion.3), kind=kLoop, calls=%fused_computation.45 | loop fusion | flops 2097152 | bytes 6291968 | tf_op jit(solution)/shard_map/convert_element_type | solution.py:151
  251.9 2.8 %reshape.239 = f32[128,4,1024]{2,1,0:T(4,128)} reshape(f32[512,1024]{1,0:T(8,128)} %get-tuple-element.67) | data formatting | bytes 4194304 | tf_op jit(solution)/shard_map/convert_element_type | solution.py:151
  254.7 1.6 reshape.240
  256.4 5.6 %multiply_reduce_fusion.1 = (f32[128,1024]{1,0:T(8,128)S(1)}, f32[128,1024]{1,0:T(8,128)S(1)}) fusion(f32[128,4,1024]{2,1,0:T(4,128)} %reshape.240, f32[128,4]{1,0:T(8,128)S(1)} %copy.167, f32[128,4,1024]{2,1,0:T(4,128)} %reshape.239), kind=kLoop, calls=%fused_computation.22 | loop fusion | flops 1835008 | bytes 5244928 | tf_op jit(solution)/shard_map/reduce_sum | solution.py:153
  262.2 1.0 add_convert_fusion
  (112 shorter events, 13.3 us)
Async XLA Ops:
  0.6 59.2 %copy-start = (bf16[1024,1024]{1,0:T(8,128)(2,1)S(1)}, bf16[1024,1024]{1,0:T(8,128)(2,1)}, u32[]{:S(2)}) copy-start(bf16[1024,1024]{1,0:T(8,128)(2,1)} %param.20) | copy-start | bytes 6291460
  0.6 17.3 %copy-start.10 = (bf16[128,1024]{1,0:T(8,128)(2,1)S(1)}, bf16[128,1024]{1,0:T(8,128)(2,1)}, u32[]{:S(2)}) copy-start(bf16[128,1024]{1,0:T(8,128)(2,1)} %param.17) | copy-start | bytes 786436
  2.6 11.8 %all-to-all-start.1 = ((bf16[128,8,128]{0,2,1:T(8,128)(2,1)}), bf16[128,8,128]{0,2,1:T(8,128)(2,1)S(1)}, u32[]{:S(2)}, u32[]{:S(2)}) async-start(bf16[128,8,128]{0,2,1:T(8,128)(2,1)} %bitcast.8), calls=%async_computation.1 | async-start | bytes 524288 | tf_op jit(solution)/shard_map/all_to_all | solution.py:76
  14.4 10.8 %all-to-all-start.2 = ((bf16[128,8,128]{0,2,1:T(8,128)(2,1)}), bf16[128,8,128]{0,2,1:T(8,128)(2,1)S(1)}, u32[]{:S(2)}, u32[]{:S(2)}) async-start(bf16[128,8,128]{0,2,1:T(8,128)(2,1)} %bitcast.10), calls=%async_computation.2 | async-start | bytes 524288 | tf_op jit(solution)/shard_map/all_to_all | solution.py:77
  25.3 10.9 %all-to-all-start = ((bf16[128,8,128]{0,2,1:T(8,128)(2,1)}), bf16[128,8,128]{0,2,1:T(8,128)(2,1)S(1)}, u32[]{:S(2)}, u32[]{:S(2)}) async-start(bf16[128,8,128]{0,2,1:T(8,128)(2,1)} %bitcast.5), calls=%async_computation | async-start | bytes 524288 | tf_op jit(solution)/shard_map/all_to_all | solution.py:75
  36.3 15.9 %copy-start.8 = (bf16[128,1024]{1,0:T(8,128)(2,1)S(1)}, bf16[128,1024]{1,0:T(8,128)(2,1)}, u32[]{:S(2)}) copy-start(bf16[128,1024]{1,0:T(8,128)(2,1)} %param.25) | copy-start | bytes 786436
  39.9 1.0 copy-start.11
  46.1 1.0 copy-start.11
  48.8 10.9 %all-to-all-start.3 = ((bf16[8,128,128]{2,1,0:T(8,128)(2,1)}), bf16[8,128,128]{2,1,0:T(8,128)(2,1)S(1)}, u32[]{:S(2)}, u32[]{:S(2)}) async-start(bf16[8,128,128]{2,1,0:T(8,128)(2,1)} %bitcast.310), calls=%async_computation.3 | async-start | bytes 524288 | tf_op jit(solution)/shard_map/all_to_all | solution.py:107
  52.2 7.6 %copy-start.12 = (bf16[128,1024]{1,0:T(8,128)(2,1)S(1)}, bf16[128,1024]{1,0:T(8,128)(2,1)}, u32[]{:S(2)}) copy-start(bf16[128,1024]{1,0:T(8,128)(2,1)} %param.16) | copy-start | bytes 786436
  55.7 5.5 %copy-start.13 = (f32[1024]{0:T(1024)S(1)}, f32[1024]{0:T(1024)}, u32[]{:S(2)}) copy-start(f32[1024]{0:T(1024)} %param.21) | copy-start | bytes 12292
  60.4 0.8 copy-start.2
  61.4 3.5 %copy-start.4 = (bf16[640,1024]{1,0:T(8,128)(2,1)S(1)}, bf16[640,1024]{1,0:T(8,128)(2,1)}, u32[]{:S(2)}) copy-start(bf16[640,1024]{1,0:T(8,128)(2,1)} %gather_fusion.2) | copy-start | bytes 3932164
  72.8 45.0 %all-to-all-start.4 = ((bf16[32,2,1,10,1024]{4,1,3,2,0:T(2,128)(2,1)}), bf16[32,2,1,10,1024]{4,1,3,2,0:T(2,128)(2,1)}, u32[]{:S(2)}, u32[]{:S(2)}) async-start(bf16[32,2,1,10,1024]{4,1,3,2,0:T(2,128)(2,1)} %copy.203), calls=%async_computation.4 | async-start | bytes 2621440 | tf_op jit(solution)/shard_map/all_to_all | solution.py:115
  117.8 38.1 %all-to-all-start.6 = ((bf16[2,32,10,1024]{3,0,2,1:T(2,128)(2,1)}), bf16[2,32,10,1024]{3,0,2,1:T(2,128)(2,1)}, u32[]{:S(2)}, u32[]{:S(2)}) async-start(bf16[2,32,10,1024]{3,0,2,1:T(2,128)(2,1)} %copy.210), calls=%async_computation.6 | async-start | bytes 2621440 | tf_op jit(solution)/shard_map/all_to_all | solution.py:120
  128.5 4.6 %copy-start.5 = (bf16[1024,2,2,512]{3,1,2,0:T(2,128)(2,1)}, bf16[1024,2,2,512]{3,1,2,0:T(2,128)(2,1)S(1)}, u32[]{:S(2)}) copy-start(bf16[1024,2,2,512]{3,1,2,0:T(2,128)(2,1)S(1)} %slice.22) | copy-start | bytes 12582916
  133.1 22.8 %copy-start.7 = (bf16[1024,2,1,512]{3,1,2,0:T(2,128)(2,1)}, bf16[1024,2,1,512]{3,1,2,0:T(2,128)(2,1)S(1)}, u32[]{:S(2)}) copy-start(bf16[1024,2,1,512]{3,1,2,0:T(2,128)(2,1)S(1)} %slice.25) | copy-start | bytes 6291460
  155.9 3.6 %copy-start.6 = (bf16[1024,2,2,512]{3,1,2,0:T(2,128)(2,1)S(1)}, bf16[1024,2,2,512]{3,1,2,0:T(2,128)(2,1)}, u32[]{:S(2)}) copy-start(bf16[1024,2,2,512]{3,1,2,0:T(2,128)(2,1)} %copy-done.5) | copy-start | bytes 12582916
  163.6 37.5 %all-to-all-start.7 = ((bf16[2,32,10,1024]{3,0,2,1:T(2,128)(2,1)}), bf16[2,32,10,1024]{3,0,2,1:T(2,128)(2,1)S(1)}, u32[]{:S(2)}, u32[]{:S(2)}) async-start(bf16[2,32,10,1024]{3,0,2,1:T(2,128)(2,1)} %bitcast.61), calls=%async_computation.7 | async-start | bytes 2621440 | tf_op jit(solution)/shard_map/all_to_all | solution.py:135
  172.5 34.2 %copy-start.14 = (f32[128,4]{0,1:T(4,128)S(1)}, f32[128,4]{0,1:T(4,128)}, u32[]{:S(2)}) copy-start(f32[128,4]{0,1:T(4,128)} %param.24) | copy-start | bytes 6148
  201.1 37.6 %all-to-all-start.5 = ((bf16[2,32,10,1024]{3,0,2,1:T(2,128)(2,1)}), bf16[2,32,10,1024]{3,0,2,1:T(2,128)(2,1)S(1)}, u32[]{:S(2)}, u32[]{:S(2)}) async-start(bf16[2,32,10,1024]{3,0,2,1:T(2,128)(2,1)} %bitcast.56), calls=%async_computation.5 | async-start | bytes 2621440 | tf_op jit(solution)/shard_map/all_to_all | solution.py:128
  256.4 5.6 %copy-start.3 = (f32[128,1024]{1,0:T(8,128)S(1)}, f32[128,1024]{1,0:T(8,128)}, u32[]{:S(2)}) copy-start(f32[128,1024]{1,0:T(8,128)} %copy-done.2) | copy-start | bytes 1572868
  256.4 5.8 %copy-start.9 = (bf16[128,1024]{1,0:T(8,128)(2,1)S(1)}, bf16[128,1024]{1,0:T(8,128)(2,1)}, u32[]{:S(2)}) copy-start(bf16[128,1024]{1,0:T(8,128)(2,1)} %param.25) | copy-start | bytes 786436
  256.4 6.8 %copy-start.1 = (bf16[1024,1024]{1,0:T(8,128)(2,1)S(1)}, bf16[1024,1024]{1,0:T(8,128)(2,1)}, u32[]{:S(2)}) copy-start(bf16[1024,1024]{1,0:T(8,128)(2,1)} %param.20) | copy-start | bytes 6291460
